TPU v7x, 32 devices: a whole 2x2x4 slice. The times are simulated.
32 devices in a mesh: doc: 4 (over z), feat: 8 (over y, x, core).
Axes of the slice: x: 2, y: 2, z: 4, core: 2. Of those that a mesh axis runs over, the one named last changes fastest.
Arguments:
- documents: bfloat16 [512, 512], P('doc', 'feat'), may hold values from -6 to 6
- directions: bfloat16 [512, 32768], P('doc', 'feat'), may hold values from -0.5 to 0.5
- phase: float32 [32768], P('feat'), may hold values from -3.140625 to 3.140625
- amplitude: float32 [32768], P('feat'), may hold values from 0.4 to 2.3
- doc_weight: float32 [512], P('doc'), may hold values from 0.5 to 4.2
- labels: int32 [512], P('doc'), may hold values from 0 to 127
Outputs:
- margins: float32 [512, 128], P('doc')
- scaled_weights: float32 [32768, 128], P('feat')
All inputs are finite; a program needn't handle non-finite values.
Results may differ from a plain program's by a relative error of at most 0.0003.
Values may be sent and summed in bfloat16 or wider, within the bound.
A program may use at most 64 MiB of HBM per device.

v0:
```python
import jax
import jax.numpy as jnp
from jax import lax
from jax.sharding import PartitionSpec as P

C = 128
ITERS = 3
NEWTON = 3
shrink_level = 0.1
ratio_floor = 1e-06


def project_tile(features, factor, start, target):
    residue = target - jnp.dot(features, start, precision=lax.Precision.HIGHEST)
    halfway = lax.linalg.triangular_solve(factor, residue, left_side=True, lower=True)
    solved = lax.linalg.triangular_solve(
        factor, halfway, left_side=True, lower=True, transpose_a=True
    )
    new_copy = start + lax.dot_general(
        features, solved, (((0,), (0,)), ((), ())), precision=lax.Precision.HIGHEST
    )
    new_part = jnp.dot(features, new_copy, precision=lax.Precision.HIGHEST)
    return (new_copy, new_part)


def logistic_prox(target, signs, weight_ratio):
    current = target
    for newton_step in range(NEWTON):
        chance = jax.nn.sigmoid(-signs * current)
        gradient = current - target - weight_ratio * signs * chance
        current = current - gradient / (1.0 + weight_ratio * chance * (1.0 - chance))
    return current


def shrink_values(target, limit):
    return target - jnp.clip(target, -limit, limit)


def per_device(documents, directions, phase, amplitude, doc_weight, labels):
    doc_full = lax.all_gather(documents, "feat", axis=1, tiled=True)
    doc_count = documents.shape[0]
    width_tile = directions.shape[1]
    num_feat = lax.axis_size("feat")
    num_doc = lax.axis_size("doc")
    angles = jnp.dot(
        doc_full,
        lax.all_gather(directions, "doc", axis=0, tiled=True),
        preferred_element_type=jnp.float32,
    )
    features = jnp.sqrt(2.0 / width_tile) * amplitude * jnp.cos(angles + phase)
    gram = jnp.eye(doc_count, dtype=jnp.float32) + lax.dot_general(
        features, features, (((1,), (1,)), ((), ())), precision=lax.Precision.HIGHEST
    )
    factor = jnp.linalg.cholesky(gram)
    signs = jnp.where(labels[:, None] == jnp.arange(C, dtype=jnp.int32)[None, :], 1.0, -1.0).astype(
        jnp.float32
    )
    share_rows = doc_count // num_feat
    offset = lax.axis_index("feat") * share_rows
    local_signs = lax.dynamic_slice_in_dim(signs, offset, share_rows, 0)
    local_weight = lax.dynamic_slice_in_dim(doc_weight, offset, share_rows, 0)[:, None]
    rho = jnp.float32(1.0)
    margins = logistic_prox(
        jnp.zeros(local_signs.shape, jnp.float32), local_signs, local_weight / rho
    )
    sums = jnp.zeros(local_signs.shape, jnp.float32)
    duals_y = jnp.zeros(local_signs.shape, jnp.float32)
    duals_x = jnp.zeros((width_tile, C), jnp.float32)
    partial_value = jnp.zeros((doc_count, C), jnp.float32)
    weights = jnp.zeros((width_tile, C), jnp.float32)
    for step in range(ITERS):
        correction = (margins - duals_y - sums) / num_feat
        correction = lax.all_gather(correction, "feat", axis=0, tiled=True)
        new_copy, partial_value = project_tile(
            features, factor, weights - duals_x, partial_value + correction
        )
        sums = lax.psum_scatter(partial_value, "feat", scatter_dimension=0, tiled=True)
        old_weights = weights
        old_margins = margins
        limit = shrink_level / (rho * num_doc)
        summed = lax.psum(new_copy + duals_x, "doc")
        weights = shrink_values(summed / num_doc, limit)
        margins = logistic_prox(sums + duals_y, local_signs, local_weight / rho)
        duals_x = duals_x + new_copy - weights
        duals_y = duals_y + sums - margins
        if step + 1 < ITERS:
            margin_gap = jnp.sum((sums - margins) ** 2)
            margin_move = jnp.sum((margins - old_margins) ** 2)
            primal, dual_norm = lax.psum(
                (
                    jnp.sum((new_copy - weights) ** 2) + margin_gap,
                    jnp.sum((weights - old_weights) ** 2) + margin_move,
                ),
                ("doc", "feat"),
            )
            dual_norm = rho * rho * dual_norm
            growth = ((primal + ratio_floor) / (dual_norm + ratio_floor)) ** 0.25
            rho = rho * growth
            duals_x = duals_x / growth
            duals_y = duals_y / growth
    margins = lax.all_gather(margins, "feat", axis=0, tiled=True)
    return (margins, num_feat * weights)


def solution(mesh):
    in_specs = (P("doc", "feat"), P("doc", "feat"), P("feat"), P("feat"), P("doc"), P("doc"))
    out_specs = (P("doc", None), P("feat", None))
    return jax.shard_map(
        per_device, mesh=mesh, in_specs=in_specs, out_specs=out_specs, check_vma=False
    )
```

profile of v0, /device:TPU:0, one launch (start us, length us, event | category | flops | bytes accessed | tf_op | source)
XLA Modules:
  0.0 668.8 jit_solution(7295771002411407596)
XLA Ops:
  9.6 10.7 %all_gather.20 = f32[128,128]{1,0:T(8,128)S(1)} all-gather(f32[16,128]{1,0:T(8,128)S(1)} %broadcast_multiply_fusion.1), channel_id=1, replica_groups=mesh['doc'=4,'feat'=8] {'feat'}, dimensions={0}, use_global_device_ids=true | all-gather | bytes 73728 | tf_op jit(solution)/shard_map/all_gather | solution.py:73
  20.3 9.2 %all_gather.18 = bf16[128,512]{0,1:T(8,128)(2,1)S(1)} all-gather(bf16[128,64]{0,1:T(8,128)(2,1)} %param.10), channel_id=1, replica_groups=mesh['doc'=4,'feat'=8] {'feat'}, dimensions={1}, use_global_device_ids=true | all-gather | bytes 147456 | tf_op jit(solution)/shard_map/all_gather | solution.py:40
  30.2 62.9 %all-gather.2.cloned.1.call-done = bf16[512,4096]{1,0:T(8,128)(2,1)} async-done(((bf16[128,4096]{1,0:T(8,128)(2,1)}), bf16[512,4096]{1,0:T(8,128)(2,1)}) %all-gather.2.cloned.1.call-update) | async-done | bytes 4194320 | tf_op jit(solution)/shard_map/all_gather | solution.py:47
  93.0 9.5 %fusion.1 = f32[128,4096]{1,0:T(8,128)S(1)} fusion(bf16[128,512]{0,1:T(8,128)(2,1)S(1)} %all_gather.18, bf16[512,4096]{1,0:T(8,128)(2,1)} %all-gather.2.cloned.1.call-done, f32[4096]{0:T(1024)} %param.12, f32[4096]{0:T(1024)S(1)} %broadcast_multiply_fusion), kind=kOutput, calls=%fused_computation.4 | convolution fusion | flops 537919488 | bytes 6455296 | tf_op jit(solution)/shard_map/dot_general | solution.py:45
  102.5 1.8 fusion.140
  104.3 1.8 convolution_subtract_fusion.2
  106.2 11.7 %cholesky.20 = f32[128,128]{1,0:T(8,128)S(1)} custom-call(f32[128,128]{1,0:T(8,128)S(1)} %fusion.22), custom_call_target="Cholesky" | custom-call | tf_op jit(solution)/shard_map/jit(cholesky)/cholesky | solution.py:54
  119.3 9.8 %custom-call.14 = f32[1,128,128]{1,2,0:T(8,128)S(1)} custom-call(f32[1,128,128]{2,1,0:T(8,128)S(1)} %fusion.8), custom_call_target="InvertDiagBlocksLowerTriangular" | custom-call | tf_op jit(solution)/shard_map/triangular_solve/custom-call.2 | solution.py:16
  129.6 16.5 %fusion.141 = f32[4096,128]{1,0:T(8,128)} fusion(f32[128,4096]{1,0:T(8,128)S(1)} %fusion.1, f32[128,128]{1,0:T(8,128)S(1)} %fusion.19), kind=kOutput, calls=%fused_computation.176 | convolution fusion | flops 805306368 | bytes 4259840 | tf_op jit(solution)/shard_map/dot_general | solution.py:19
  146.1 4.4 fusion.142
  151.2 31.4 %reduce-scatter.4.cloned.1.call-done = f32[16,128]{1,0:T(8,128)} async-done(((f32[128,128]{1,0:T(8,128)}), f32[16,128]{1,0:T(8,128)}) %reduce-scatter.4.cloned.1.call-update) | async-done | bytes 8208 | tf_op jit(solution)/shard_map/reduce_scatter | solution.py:77
  182.6 1.5 multiply_reduce_fusion.6
  185.5 86.3 %all-reduce.6.cloned.1.call-done = f32[4096,128]{1,0:T(8,128)} async-done(((f32[4096,128]{1,0:T(8,128)}), f32[4096,128]{1,0:T(8,128)}) %all-reduce.6.cloned.1.call-update) | async-done | bytes 2097168 | tf_op jit(solution)/shard_map/psum | solution.py:81
  271.8 3.4 multiply_reduce_fusion.2
  277.5 39.3 %all-reduce.1 = (f32[]{:T(128)}, f32[]{:T(128)}) all-reduce(f32[]{:T(128)S(6)} %add.189, f32[]{:T(128)S(6)} %add.191), channel_id=1, replica_groups=mesh['doc'=4,'feat'=8] {'doc','feat'}, use_global_device_ids=true, to_apply=%region_6.9 | all-reduce | flops 2 | bytes 16 | tf_op jit(solution)/shard_map/psum | solution.py:89
  318.2 10.2 %all_gather.21 = f32[128,128]{1,0:T(8,128)S(1)} all-gather(f32[16,128]{1,0:T(8,128)S(1)} %subtract_multiply_fusion.2), channel_id=1, replica_groups=mesh['doc'=4,'feat'=8] {'feat'}, dimensions={0}, use_global_device_ids=true | all-gather | bytes 73728 | tf_op jit(solution)/shard_map/all_gather | solution.py:73
  328.4 4.9 convolution_subtract_fusion.1
  333.8 5.1 fusion.5
  340.2 2.8 fusion.143
  343.8 31.9 %reduce-scatter.6.cloned.1.call-done = f32[16,128]{1,0:T(8,128)} async-done(((f32[128,128]{1,0:T(8,128)}), f32[16,128]{1,0:T(8,128)}) %reduce-scatter.6.cloned.1.call-update) | async-done | bytes 8208 | tf_op jit(solution)/shard_map/reduce_scatter | solution.py:77
  375.7 1.5 multiply_reduce_fusion.4
  377.2 87.4 %all-reduce.8.cloned.1.call-done = f32[4096,128]{1,0:T(8,128)} async-done(((f32[4096,128]{1,0:T(8,128)}), f32[4096,128]{1,0:T(8,128)}) %all-reduce.8.cloned.1.call-update) | async-done | bytes 2097168 | tf_op jit(solution)/shard_map/psum | solution.py:81
  464.7 4.4 multiply_reduce_fusion
  471.5 39.3 %all-reduce = (f32[]{:T(128)}, f32[]{:T(128)}) all-reduce(f32[]{:T(128)S(6)} %add.203, f32[]{:T(128)S(6)} %add.205), channel_id=1, replica_groups=mesh['doc'=4,'feat'=8] {'doc','feat'}, use_global_device_ids=true, to_apply=%region_14.17 | all-reduce | flops 2 | bytes 16 | tf_op jit(solution)/shard_map/psum | solution.py:89
  512.2 10.5 %all_gather.22 = f32[128,128]{1,0:T(8,128)S(1)} all-gather(f32[16,128]{1,0:T(8,128)S(1)} %subtract_multiply_fusion.1), channel_id=1, replica_groups=mesh['doc'=4,'feat'=8] {'feat'}, dimensions={0}, use_global_device_ids=true | all-gather | bytes 73728 | tf_op jit(solution)/shard_map/all_gather | solution.py:73
  522.7 5.0 convolution_subtract_fusion
  528.2 5.1 fusion.6
  533.3 2.8 fusion.144
  537.0 31.8 %reduce-scatter.8.cloned.1.call-done = f32[16,128]{1,0:T(8,128)} async-done(((f32[128,128]{1,0:T(8,128)}), f32[16,128]{1,0:T(8,128)}) %reduce-scatter.8.cloned.1.call-update) | async-done | bytes 8208 | tf_op jit(solution)/shard_map/reduce_scatter | solution.py:77
  569.6 9.2 %all_gather.23 = f32[128,128]{1,0:T(8,128)S(1)} all-gather(f32[16,128]{1,0:T(8,128)S(1)} %fusion.64), channel_id=1, replica_groups=mesh['doc'=4,'feat'=8] {'feat'}, dimensions={0}, use_global_device_ids=true | all-gather | bytes 73728 | tf_op jit(solution)/shard_map/all_gather | solution.py:101
  578.8 79.0 %all-reduce.10.cloned.1.call-done = f32[4096,128]{1,0:T(8,128)} async-done(((f32[4096,128]{1,0:T(8,128)}), f32[4096,128]{1,0:T(8,128)}) %all-reduce.10.cloned.1.call-update) | async-done | bytes 2097168 | tf_op jit(solution)/shard_map/psum | solution.py:81
  657.9 3.2 subtract_multiply_fusion
  (56 shorter events, 12.5 us)
Async XLA Ops:
  7.2 85.9 %all-gather.2.cloned.1.call-start = ((), (), s32[]{:S(2)}) async-start(), calls=%async_computation.3 | async-start | bytes 5242880 | tf_op jit(solution)/shard_map/all_gather | solution.py:47
  7.9 174.7 %reduce-scatter.4.cloned.1.call-start = ((), (), s32[]{:S(2)}) async-start(), calls=%async_computation.5 | async-start | bytes 73728 | tf_op jit(solution)/shard_map/reduce_scatter | solution.py:77
  150.5 121.3 %all-reduce.6.cloned.1.call-start = ((), (), s32[]{:S(2)}) async-start(), calls=%async_computation.4 | async-start | bytes 4194304 | tf_op jit(solution)/shard_map/psum | solution.py:81
  151.2 224.5 %reduce-scatter.6.cloned.1.call-start = ((), (), s32[]{:S(2)}) async-start(), calls=%async_computation.7 | async-start | bytes 73728 | tf_op jit(solution)/shard_map/reduce_scatter | solution.py:77
  185.5 132.7 %copy-start.8 = (f32[16,128]{1,0:T(8,128)S(1)}, f32[16,128]{1,0:T(8,128)}, u32[]{:S(2)}) copy-start(f32[16,128]{1,0:T(8,128)} %reduce-scatter.4.cloned.1.call-done) | copy-start | bytes 24580
  185.5 142.9 %copy-start.6 = (f32[128,128]{1,0:T(8,128)S(1)}, f32[128,128]{1,0:T(8,128)}, u32[]{:S(2)}) copy-start(f32[128,128]{1,0:T(8,128)} %fusion.142) | copy-start | bytes 196612
  328.4 5.4 copy-start
  328.4 5.4 copy-start.1
  338.9 1.3 copy-start.2
  343.0 0.7 copy-start.9
  343.0 121.6 %all-reduce.8.cloned.1.call-start = ((), (), s32[]{:S(2)}) async-start(), calls=%async_computation.6 | async-start | bytes 4194304 | tf_op jit(solution)/shard_map/psum | solution.py:81
  343.6 225.2 %reduce-scatter.8.cloned.1.call-start = ((), (), s32[]{:S(2)}) async-start(), calls=%async_computation.8 | async-start | bytes 73728 | tf_op jit(solution)/shard_map/reduce_scatter | solution.py:77
  377.2 135.0 %copy-start.7 = (f32[16,128]{1,0:T(8,128)S(1)}, f32[16,128]{1,0:T(8,128)}, u32[]{:S(2)}) copy-start(f32[16,128]{1,0:T(8,128)} %reduce-scatter.6.cloned.1.call-done) | copy-start | bytes 24580
  377.2 145.4 %copy-start.5 = (f32[128,128]{1,0:T(8,128)S(1)}, f32[128,128]{1,0:T(8,128)}, u32[]{:S(2)}) copy-start(f32[128,128]{1,0:T(8,128)} %fusion.143) | copy-start | bytes 196612
  522.7 5.5 copy-start.3
  522.7 5.5 copy-start.4
  536.1 121.8 %all-reduce.10.cloned.1.call-start = ((), (), s32[]{:S(2)}) async-start(), calls=%async_computation.9 | async-start | bytes 4194304 | tf_op jit(solution)/shard_map/psum | solution.py:81
Sparse Core Ops, SparseCore 0:
  9.5 83.4 all-gather.1
  150.6 32.0 reduce-scatter.3
  185.6 86.1 all-reduce.5
  343.2 32.5 reduce-scatter.5
  378.5 86.0 all-reduce.7
  536.2 32.5 reduce-scatter.7
  571.7 86.0 all-reduce.9
where the time goes:
time: 673 us; the launch traced here: 669 us
  waiting for transfers between devices  413 us (61%)
  blocking collectives  128 us (19%)
  matrix products  61 us (9%)
  other arithmetic  40.1 us (6%)
  between operations  22.2 us (3%)
    psum x3, waiting for transfers between devices, per_device(): summed = lax.psum(new_copy + duals_x, 'doc')  253 us
    reduce_scatter x3, waiting for transfers between devices, per_device(): lax.psum_scatter(partial_value, 'feat', scatter_dimension=0, tiled=True)  95.1 us
    psum x2, blocking collectives, per_device(): lax.psum((jnp.sum((new_copy - weights) ** 2) + margin_gap, jnp.sum((weigh...  78.6 us
    all_gather x1, waiting for transfers between devices, per_device(): lax.all_gather(directions, 'doc', axis=0, tiled=True)  62.9 us
    all_gather x3, blocking collectives, per_device(): correction = lax.all_gather(correction, 'feat', axis=0, tiled=True)  31.4 us
    dot_general x3, matrix products, project_tile(): lax.dot_general(features, solved, (((0,), (0,)), ((), ())), precision=lax...  26.6 us
  transfers between devices with their start and end apart: 7, of which 7 were waited for; matrix products, arithmetic and copies ran while one was open for 1% of the time, Pallas kernels for 0%

commit v1 on v0

--- a/solution.py
+++ b/solution.py
@@ -8,6 +8,18 @@
 NEWTON = 3
 shrink_level = 0.1
 ratio_floor = 1e-06
+
+
+def doubled_up(x, axis, dim):
+    ways, here, step = (lax.axis_size(axis), lax.axis_index(axis), x.shape[dim])
+    line, have = (x, 1)
+    while have < ways:
+        line = jnp.concatenate(
+            [line, lax.ppermute(line, axis, [(d, (d - have) % ways) for d in range(ways)])],
+            axis=dim,
+        )
+        have = 2 * have
+    return jnp.roll(line, here * step, axis=dim)
 
 
 def project_tile(features, factor, start, target):
@@ -42,11 +54,7 @@
     width_tile = directions.shape[1]
     num_feat = lax.axis_size("feat")
     num_doc = lax.axis_size("doc")
-    angles = jnp.dot(
-        doc_full,
-        lax.all_gather(directions, "doc", axis=0, tiled=True),
-        preferred_element_type=jnp.float32,
-    )
+    angles = jnp.dot(doc_full, doubled_up(directions, "doc", 0), preferred_element_type=jnp.float32)
     features = jnp.sqrt(2.0 / width_tile) * amplitude * jnp.cos(angles + phase)
     gram = jnp.eye(doc_count, dtype=jnp.float32) + lax.dot_general(
         features, features, (((1,), (1,)), ((), ())), precision=lax.Precision.HIGHEST

time: 673 us -> 613 us (0.911)
  waiting for transfers between devices: 413 us -> 346 us
    psum x3, waiting for transfers between devices: 253 us -> 153 us  [per_device(): summed = lax.psum(new_copy + duals_x, 'doc')]
    ppermute x0 -> x2, waiting for transfers between devices: none -> 95.1 us  [doubled_up(): lax.ppermute(line, axis, [(d, (d - have) % ways) for d in range(ways)])]
    all_gather x1 -> x0, waiting for transfers between devices: 62.9 us -> none  [per_device(): lax.all_gather(directions, 'doc', axis=0, tiled=True)]
    dot_general x3, matrix products: 26.6 us -> 10.1 us  [project_tile(): lax.dot_general(features, solved, (((0,), (0,)), ((), ())), precision=lax...]
  transfers between devices with their start and end apart: 7 -> 8, of which waited for: 7 -> 8; matrix products, arithmetic and copies ran while one was open for 1% -> 1% of each run, Pallas kernels for 0% -> 0%
where the time goes in v1:
time: 613 us; the launch traced here: 609 us
  waiting for transfers between devices  346 us (56%)
  blocking collectives  127 us (21%)
  matrix products  56.8 us (9%)
  other arithmetic  42.1 us (7%)
  between operations  23.8 us (4%)
  starting transfers between devices  6.75 us (1%)
    psum x3, waiting for transfers between devices, per_device(): summed = lax.psum(new_copy + duals_x, 'doc')  153 us
    reduce_scatter x3, waiting for transfers between devices, per_device(): lax.psum_scatter(partial_value, 'feat', scatter_dimension=0, tiled=True)  96.9 us
    ppermute x2, waiting for transfers between devices, doubled_up(): lax.ppermute(line, axis, [(d, (d - have) % ways) for d in range(ways)])  95.1 us
    psum x2, blocking collectives, per_device(): lax.psum((jnp.sum((new_copy - weights) ** 2) + margin_gap, jnp.sum((weigh...  78.8 us
    all_gather x3, blocking collectives, per_device(): correction = lax.all_gather(correction, 'feat', axis=0, tiled=True)  30 us
    dot_general x3, matrix products, project_tile(): residue = target - jnp.dot(features, start, precision=lax.Precision.HIGHEST)  16 us
    dot_general x3, matrix products, project_tile(): new_part = jnp.dot(features, new_copy, precision=lax.Precision.HIGHEST)  13.9 us
    another operation x3, other arithmetic, per_device(): factor = jnp.linalg.cholesky(gram)  12.4 us
  transfers between devices with their start and end apart: 8, of which 8 were waited for; matrix products, arithmetic and copies ran while one was open for 1% of the time, Pallas kernels for 0%

profile of v1, /device:TPU:0, one launch (start us, length us, event | category | flops | bytes accessed | tf_op | source)
XLA Modules:
  0.0 609.1 jit_solution(15982903735560898293)
XLA Ops:
  8.1 5.1 collective-permute-start
  13.2 22.7 %collective-permute-done = bf16[128,4096]{1,0:T(8,128)(2,1)S(1)} collective-permute-done((bf16[128,4096]{1,0:T(8,128)(2,1)}, bf16[128,4096]{1,0:T(8,128)(2,1)S(1)}, u32[]{:S(2)}, u32[]{:S(2)}) %collective-permute-start) | collective-permute-done | bytes 1048608 | tf_op jit(solution)/shard_map/ppermute | solution.py:18
  40.4 9.3 %all_gather.16 = f32[128,128]{1,0:T(8,128)S(1)} all-gather(f32[16,128]{1,0:T(8,128)S(1)} %broadcast_multiply_fusion.1), channel_id=1, replica_groups=mesh['doc'=4,'feat'=8] {'feat'}, dimensions={0}, use_global_device_ids=true | all-gather | bytes 73728 | tf_op jit(solution)/shard_map/all_gather | solution.py:81
  49.6 9.2 %all_gather.15 = bf16[128,512]{0,1:T(8,128)(2,1)S(1)} all-gather(bf16[128,64]{0,1:T(8,128)(2,1)S(1)} %copy-done.11), channel_id=1, replica_groups=mesh['doc'=4,'feat'=8] {'feat'}, dimensions={1}, use_global_device_ids=true | all-gather | bytes 147456 | tf_op jit(solution)/shard_map/all_gather | solution.py:52
  59.0 72.4 %collective-permute-done.1 = bf16[256,4096]{1,0:T(8,128)(2,1)} collective-permute-done((bf16[256,4096]{1,0:T(8,128)(2,1)}, bf16[256,4096]{1,0:T(8,128)(2,1)}, u32[]{:S(2)}, u32[]{:S(2)}) %collective-permute-start.1) | collective-permute-done | bytes 2097184 | tf_op jit(solution)/shard_map/ppermute | solution.py:18
  135.0 11.8 %fusion.1 = f32[4096,128]{1,0:T(8,128)S(1)} fusion(bf16[128,512]{0,1:T(8,128)(2,1)S(1)} %all_gather.15, bf16[1024,4096]{1,0:T(8,128)(2,1)S(1)} %constant_dynamic-update-slice_fusion, s32[]{:T(128)S(6)} %select_n.26, f32[4096]{0:T(1024)S(1)} %copy-done.10, f32[4096]{0:T(1024)S(1)} %broadcast_multiply_fusion), kind=kOutput, calls=%fused_computation.4 | convolution fusion | flops 537919488 | bytes 6455300 | tf_op jit(solution)/shard_map/dot_general | solution.py:57
  146.9 3.5 fusion.142
  150.5 11.7 %cholesky.20 = f32[128,128]{1,0:T(8,128)S(1)} custom-call(f32[128,128]{1,0:T(8,128)S(1)} %fusion.23), custom_call_target="Cholesky" | custom-call | tf_op jit(solution)/shard_map/jit(cholesky)/cholesky | solution.py:62
  163.5 9.8 %custom-call.14 = f32[1,128,128]{1,2,0:T(8,128)S(1)} custom-call(f32[1,128,128]{2,1,0:T(8,128)S(1)} %fusion.9), custom_call_target="InvertDiagBlocksLowerTriangular" | custom-call | tf_op jit(solution)/shard_map/triangular_solve/custom-call.2 | solution.py:28
  173.3 3.6 convolution_subtract_fusion.2
  177.4 3.1 fusion.143
  180.5 5.7 fusion.144
  186.9 33.0 %reduce-scatter.4.cloned.1.call-done = f32[16,128]{1,0:T(8,128)} async-done(((f32[128,128]{1,0:T(8,128)}), f32[16,128]{1,0:T(8,128)}) %reduce-scatter.4.cloned.1.call-update) | async-done | bytes 8208 | tf_op jit(solution)/shard_map/reduce_scatter | solution.py:85
  222.6 53.0 %all-reduce.6.cloned.1.call-done = f32[4096,128]{1,0:T(8,128)} async-done(((f32[4096,128]{1,0:T(8,128)}), f32[4096,128]{1,0:T(8,128)}) %all-reduce.6.cloned.1.call-update) | async-done | bytes 2097168 | tf_op jit(solution)/shard_map/psum | solution.py:89
  275.6 3.4 multiply_reduce_fusion.2
  281.4 39.3 %all-reduce.1 = (f32[]{:T(128)}, f32[]{:T(128)}) all-reduce(f32[]{:T(128)S(6)} %add.202, f32[]{:T(128)S(6)} %add.204), channel_id=1, replica_groups=mesh['doc'=4,'feat'=8] {'doc','feat'}, use_global_device_ids=true, to_apply=%region_6.9 | all-reduce | flops 2 | bytes 16 | tf_op jit(solution)/shard_map/psum | solution.py:97
  322.0 10.4 %all_gather.17 = f32[128,128]{1,0:T(8,128)S(1)} all-gather(f32[16,128]{1,0:T(8,128)S(1)} %subtract_multiply_fusion.2), channel_id=1, replica_groups=mesh['doc'=4,'feat'=8] {'feat'}, dimensions={0}, use_global_device_ids=true | all-gather | bytes 73728 | tf_op jit(solution)/shard_map/all_gather | solution.py:81
  332.5 6.2 %convolution_subtract_fusion.1 = f32[128,128]{1,0:T(8,128)S(1)} fusion(f32[4096,128]{1,0:T(8,128)S(1)} %fusion.1, f32[128,128]{1,0:T(8,128)S(1)} %copy-done.7, f32[128,128]{1,0:T(8,128)S(1)} %all_gather.17, f32[4096,128]{1,0:T(8,128)} %all-reduce.6.cloned.1.call-done, f32[]{:T(128)S(6)} %pow.6, f32[4096,128]{1,0:T(8,128)} %fusion.143), kind=kOutput, calls=%fused_computation.16 | convolution fusion | flops 808484864 | bytes 6488068 | tf_op jit(solution)/shard_map/dot_general | solution.py:26
  339.2 3.5 fusion.6
  344.0 4.1 fusion.145
  348.9 31.9 %reduce-scatter.6.cloned.1.call-done = f32[16,128]{1,0:T(8,128)} async-done(((f32[128,128]{1,0:T(8,128)}), f32[16,128]{1,0:T(8,128)}) %reduce-scatter.6.cloned.1.call-update) | async-done | bytes 8208 | tf_op jit(solution)/shard_map/reduce_scatter | solution.py:85
  382.3 54.2 %all-reduce.8.cloned.1.call-done = f32[4096,128]{1,0:T(8,128)} async-done(((f32[4096,128]{1,0:T(8,128)}), f32[4096,128]{1,0:T(8,128)}) %all-reduce.8.cloned.1.call-update) | async-done | bytes 2097168 | tf_op jit(solution)/shard_map/psum | solution.py:89
  436.5 4.4 multiply_reduce_fusion
  443.4 39.5 %all-reduce = (f32[]{:T(128)}, f32[]{:T(128)}) all-reduce(f32[]{:T(128)S(6)} %add.216, f32[]{:T(128)S(6)} %add.218), channel_id=1, replica_groups=mesh['doc'=4,'feat'=8] {'doc','feat'}, use_global_device_ids=true, to_apply=%region_14.17 | all-reduce | flops 2 | bytes 16 | tf_op jit(solution)/shard_map/psum | solution.py:97
  484.3 10.3 %all_gather.18 = f32[128,128]{1,0:T(8,128)S(1)} all-gather(f32[16,128]{1,0:T(8,128)S(1)} %subtract_multiply_fusion.1), channel_id=1, replica_groups=mesh['doc'=4,'feat'=8] {'feat'}, dimensions={0}, use_global_device_ids=true | all-gather | bytes 73728 | tf_op jit(solution)/shard_map/all_gather | solution.py:81
  494.6 6.2 %convolution_subtract_fusion = f32[128,128]{1,0:T(8,128)S(1)} fusion(f32[4096,128]{1,0:T(8,128)S(1)} %fusion.1, f32[128,128]{1,0:T(8,128)S(1)} %copy-done.6, f32[128,128]{1,0:T(8,128)S(1)} %all_gather.18, f32[]{:T(128)S(6)} %pow.7, f32[4096,128]{1,0:T(8,128)} %get-tuple-element.19, f32[]{:T(128)S(6)} %neg.63, f32[]{:T(128)S(6)} %div.173, ...), kind=kOutput, calls=%fused_computation.15 | convolution fusion | flops 809009152 | bytes 6488076 | tf_op jit(solution)/shard_map/dot_general | solution.py:26
  501.4 3.5 fusion.7
  504.9 4.1 fusion.146
  509.7 32.0 %reduce-scatter.8.cloned.1.call-done = f32[16,128]{1,0:T(8,128)} async-done(((f32[128,128]{1,0:T(8,128)}), f32[16,128]{1,0:T(8,128)}) %reduce-scatter.8.cloned.1.call-update) | async-done | bytes 8208 | tf_op jit(solution)/shard_map/reduce_scatter | solution.py:85
  542.6 9.2 %all_gather.19 = f32[128,128]{1,0:T(8,128)S(1)} all-gather(f32[16,128]{1,0:T(8,128)S(1)} %fusion.65), channel_id=1, replica_groups=mesh['doc'=4,'feat'=8] {'feat'}, dimensions={0}, use_global_device_ids=true | all-gather | bytes 73728 | tf_op jit(solution)/shard_map/all_gather | solution.py:109
  551.8 45.7 %all-reduce.10.cloned.1.call-done = f32[4096,128]{1,0:T(8,128)} async-done(((f32[4096,128]{1,0:T(8,128)}), f32[4096,128]{1,0:T(8,128)}) %all-reduce.10.cloned.1.call-update) | async-done | bytes 2097168 | tf_op jit(solution)/shard_map/psum | solution.py:89
  597.4 3.2 subtract_multiply_fusion
  (74 shorter events, 20.2 us)
Async XLA Ops:
  8.0 50.8 %copy-start.3 = (bf16[128,4096]{1,0:T(8,128)(2,1)S(1)}, bf16[128,4096]{1,0:T(8,128)(2,1)}, u32[]{:S(2)}) copy-start(bf16[128,4096]{1,0:T(8,128)(2,1)} %param.11) | copy-start | bytes 3145732
  8.0 32.1 %copy-start.14 = (s32[128]{0:T(128)S(1)}, s32[128]{0:T(128)}, u32[]{:S(2)}) copy-start(s32[128]{0:T(128)} %param.15) | copy-start | bytes 1540
  8.0 32.1 %copy-start.13 = (f32[128]{0:T(128)S(1)}, f32[128]{0:T(128)}, u32[]{:S(2)}) copy-start(f32[128]{0:T(128)} %param.14) | copy-start | bytes 1540
  8.0 41.6 %copy-start.11 = (bf16[128,64]{0,1:T(8,128)(2,1)S(1)}, bf16[128,64]{0,1:T(8,128)(2,1)}, u32[]{:S(2)}) copy-start(bf16[128,64]{0,1:T(8,128)(2,1)} %param.10) | copy-start | bytes 49156
  8.0 50.8 %copy-start.12 = (f32[4096]{0:T(1024)S(1)}, f32[4096]{0:T(1024)}, u32[]{:S(2)}) copy-start(f32[4096]{0:T(1024)} %param.13) | copy-start | bytes 49156
  8.0 211.8 %reduce-scatter.4.cloned.1.call-start = ((), (), s32[]{:S(2)}) async-start(), calls=%async_computation.4 | async-start | bytes 73728 | tf_op jit(solution)/shard_map/reduce_scatter | solution.py:85
  8.1 27.9 %collective-permute-start = (bf16[128,4096]{1,0:T(8,128)(2,1)}, bf16[128,4096]{1,0:T(8,128)(2,1)S(1)}, u32[]{:S(2)}, u32[]{:S(2)}) collective-permute-start(bf16[128,4096]{1,0:T(8,128)(2,1)} %param.11), channel_id=1, source_target_pairs={{0,24},{8,0},{16,8},{24,16},{1,25},{9,1},{17,9},{25,17},{2,26},{10... | collective-permute-start | bytes 3145736 | tf_op jit(solution)/shard_map/ppermute | solution.py:18
  38.7 92.7 %collective-permute-start.1 = (bf16[256,4096]{1,0:T(8,128)(2,1)}, bf16[256,4096]{1,0:T(8,128)(2,1)}, u32[]{:S(2)}, u32[]{:S(2)}) collective-permute-start(bf16[256,4096]{1,0:T(8,128)(2,1)} %pad_maximum_fusion), channel_id=1, source_target_pairs={{0,16},{8,24},{16,0},{24,8},{1,17},{9,25},{17,1},{25,9},{2,18},{10... | collective-permute-start | bytes 6291464 | tf_op jit(solution)/shard_map/ppermute | solution.py:18
  133.3 1.8 copy-start.10
  186.2 89.3 %all-reduce.6.cloned.1.call-start = ((), (), s32[]{:S(2)}) async-start(), calls=%async_computation.3 | async-start | bytes 4194304 | tf_op jit(solution)/shard_map/psum | solution.py:89
  186.8 194.0 %reduce-scatter.6.cloned.1.call-start = ((), (), s32[]{:S(2)}) async-start(), calls=%async_computation.6 | async-start | bytes 73728 | tf_op jit(solution)/shard_map/reduce_scatter | solution.py:85
  222.6 99.4 %copy-start.9 = (f32[16,128]{1,0:T(8,128)S(1)}, f32[16,128]{1,0:T(8,128)}, u32[]{:S(2)}) copy-start(f32[16,128]{1,0:T(8,128)} %reduce-scatter.4.cloned.1.call-done) | copy-start | bytes 24580
  222.6 109.9 %copy-start.7 = (f32[128,128]{1,0:T(8,128)S(1)}, f32[128,128]{1,0:T(8,128)}, u32[]{:S(2)}) copy-start(f32[128,128]{1,0:T(8,128)} %fusion.144) | copy-start | bytes 196612
  332.5 6.7 %copy-start = (f32[4096,128]{1,0:T(8,128)S(1)}, f32[4096,128]{1,0:T(8,128)}, u32[]{:S(2)}) copy-start(f32[4096,128]{1,0:T(8,128)} %fusion.143) | copy-start | bytes 6291460
  332.5 6.7 %copy-start.1 = (f32[4096,128]{1,0:T(8,128)S(1)}, f32[4096,128]{1,0:T(8,128)}, u32[]{:S(2)}) copy-start(f32[4096,128]{1,0:T(8,128)} %all-reduce.6.cloned.1.call-done) | copy-start | bytes 6291460
  342.6 1.3 copy-start.2
  348.1 88.4 %all-reduce.8.cloned.1.call-start = ((), (), s32[]{:S(2)}) async-start(), calls=%async_computation.5 | async-start | bytes 4194304 | tf_op jit(solution)/shard_map/psum | solution.py:89
  348.7 193.0 %reduce-scatter.8.cloned.1.call-start = ((), (), s32[]{:S(2)}) async-start(), calls=%async_computation.7 | async-start | bytes 73728 | tf_op jit(solution)/shard_map/reduce_scatter | solution.py:85
  382.3 102.0 %copy-start.8 = (f32[16,128]{1,0:T(8,128)S(1)}, f32[16,128]{1,0:T(8,128)}, u32[]{:S(2)}) copy-start(f32[16,128]{1,0:T(8,128)} %reduce-scatter.6.cloned.1.call-done) | copy-start | bytes 24580
  382.3 112.3 %copy-start.6 = (f32[128,128]{1,0:T(8,128)S(1)}, f32[128,128]{1,0:T(8,128)}, u32[]{:S(2)}) copy-start(f32[128,128]{1,0:T(8,128)} %fusion.145) | copy-start | bytes 196612
  494.6 6.8 %copy-start.4 = (f32[4096,128]{1,0:T(8,128)S(1)}, f32[4096,128]{1,0:T(8,128)}, u32[]{:S(2)}) copy-start(f32[4096,128]{1,0:T(8,128)} %get-tuple-element.19) | copy-start | bytes 6291460
  494.6 6.8 %copy-start.5 = (f32[4096,128]{1,0:T(8,128)S(1)}, f32[4096,128]{1,0:T(8,128)}, u32[]{:S(2)}) copy-start(f32[4096,128]{1,0:T(8,128)} %all-reduce.8.cloned.1.call-done) | copy-start | bytes 6291460
  509.0 88.4 %all-reduce.10.cloned.1.call-start = ((), (), s32[]{:S(2)}) async-start(), calls=%async_computation.8 | async-start | bytes 4194304 | tf_op jit(solution)/shard_map/psum | solution.py:89
Sparse Core Ops, SparseCore 0:
  186.4 33.4 reduce-scatter.3
  348.2 32.5 reduce-scatter.5
  509.2 32.5 reduce-scatter.7
Sparse Core Ops, SparseCore 1:
  189.7 85.8 all-reduce.5
  351.5 84.9 all-reduce.7
  512.4 84.9 all-reduce.9
